TPU v7x, 32 devices: a whole 2x2x4 slice. The times are simulated.
32 devices in a mesh: groups: 2 (over y), space: 4 (over x, core), chan: 4 (over z).
Axes of the slice: x: 2, y: 2, z: 4, core: 2. Of those that a mesh axis runs over, the one named last changes fastest.
Arguments:
- fields: bfloat16 [1024, 16, 256], P('chan', ('groups', 'space')), parts along dimension 1, may hold values from -6 to 6
- conv_weight: bfloat16 [27, 1024, 1024], P(None, 'chan', 'space'), may hold values from -0.0390625 to 0.0390625
Outputs:
- convolved: bfloat16 [1024, 16, 256], P('chan', ('groups', 'space')), parts along dimension 1
There are 2 independent parts, one for each index of `groups`. A program takes and returns all parts, laid end to end along the dimension named above; an argument that names none is the same for every part. Nothing has to cross between parts.
All inputs are finite; a program needn't handle non-finite values.
Results may differ from a plain program's by a relative error of at most 0.001.
Values may be sent and summed in bfloat16 or wider, within the bound.
A program may use at most 128 MiB of HBM per device.

v0:
```python
import jax
import jax.numpy as jnp
from jax import lax
from jax.sharding import PartitionSpec as P

NY = 16
NZ = 16


def padded_2(block, sides, width):
    for axis, dim in sides:
        count = lax.axis_size(axis)
        forward = [(i, i + 1) for i in range(count - 1)]
        backward = [(target, source) for source, target in forward]
        low = lax.ppermute(
            lax.slice_in_dim(block, block.shape[dim] - width, None, axis=dim), axis, forward
        )
        high = lax.ppermute(lax.slice_in_dim(block, 0, width, axis=dim), axis, backward)
        block = jnp.concatenate([low, block, high], axis=dim)
    return block


def convolve_block(summed, block, weights):
    count = block.shape[0]
    depth = block.shape[1] - 2
    shaped = block.reshape(count, depth + 2, NY, NZ)
    padded = jnp.pad(shaped, ((0, 0), (0, 0), (1, 1), (1, 1)))
    for step_x in range(3):
        for step_y in range(3):
            for step_z in range(3):
                window = padded[
                    :, step_x : step_x + depth, step_y : step_y + NY, step_z : step_z + NZ
                ].reshape(count, depth * NY * NZ)
                summed = summed + jnp.dot(
                    weights[9 * step_x + 3 * step_y + step_z],
                    window,
                    preferred_element_type=jnp.float32,
                )
    return summed


def local(fields, conv_weight):
    depth = fields.shape[1]
    owned = conv_weight.shape[1]
    weights = lax.all_gather(conv_weight, "space", axis=2, tiled=True)
    empty = jnp.zeros((owned, depth * NY * NZ), jnp.float32)
    gathered = lax.all_gather(fields, "chan", axis=0, tiled=True)
    framed = padded_2(gathered, (("space", 1),), 1)
    summed = convolve_block(empty, framed, weights)
    return summed.reshape(owned, depth, NY * NZ).astype(jnp.bfloat16)


def solution(mesh):
    return jax.shard_map(
        local,
        mesh=mesh,
        in_specs=(P("chan", ("groups", "space"), None), P(None, "chan", "space")),
        out_specs=P("chan", ("groups", "space"), None),
        check_vma=False,
    )
```

profile of v0, /device:TPU:0, one launch (start us, length us, event | category | flops | bytes accessed | tf_op | source)
XLA Modules:
  0.0 168.2 jit_solution(9444668171630820183)
XLA Ops:
  6.5 0.0 all-gather.3.cloned.1.call-start
  6.5 1.8 %copy.4 = bf16[256,2,256]{0,2,1:T(8,128)(2,1)} copy(bf16[256,2,256]{2,1,0:T(2,128)(2,1)} %param.2) | data formatting | bytes 524288 | tf_op args[0]
  8.3 0.0 all-gather.3.cloned.1.call-update
  8.4 0.0 all-gather.5.cloned.1.call-start
  8.4 0.7 all-gather.5.cloned.1.call-update
  9.1 32.5 %all-gather.3.cloned.1.call-done = bf16[1024,2,256]{0,2,1:T(8,128)(2,1)} async-done(((bf16[256,2,256]{0,2,1:T(8,128)(2,1)}), bf16[1024,2,256]{0,2,1:T(8,128)(2,1)}) %all-gather.3.cloned.1.call-update) | async-done | bytes 1048592 | tf_op jit(solution)/shard_map/all_gather | solution.py:47
  41.6 1.3 fusion.13
  42.9 1.3 collective-permute-start.1
  44.1 3.1 %collective-permute-start = (bf16[1024,1,256]{0,2,1:T(8,128)(2,1)S(1)}, bf16[1024,1,256]{0,2,1:T(8,128)(2,1)S(1)}, u32[]{:S(2)}, u32[]{:S(2)}) collective-permute-start(bf16[1024,1,256]{0,2,1:T(8,128)(2,1)S(1)} %get-tuple-element.32), channel_id=1, source_target_pairs={{0,4},{4,8},{8,12},{1,5},{5,9},{9,13},{2,6},{6,10},{10,14},{3,7},{... | collective-permute-start | bytes 1572872 | tf_op jit(solution)/shard_map/ppermute | solution.py:15
  47.2 0.0 collective-permute-done.1
  47.2 1.5 collective-permute-done
  48.7 1.6 pad_maximum_fusion
  50.3 3.4 %pad_slice_fusion.1 = (bf16[1024,2,16,16]{0,3,2,1:T(8,128)(2,1)S(1)}, bf16[1024,2,16,16]{0,3,2,1:T(8,128)(2,1)}, bf16[1024,2,16,16]{0,3,2,1:T(8,128)(2,1)S(1)}, ...) fusion(bf16[1024,4,16,16]{0,3,2,1:T(8,128)(2,1)S(1)} %bitcast.181), kind=kLoop, calls=%fused_computation.1 | loop fusion | bytes 13631488 | tf_op jit(solution)/shard_map/slice | solution.py:31
  53.7 7.4 %pad_slice_fusion = (bf16[1024,2,16,16]{0,3,2,1:T(8,128)(2,1)}, bf16[1024,2,16,16]{0,3,2,1:T(8,128)(2,1)}, bf16[1024,2,16,16]{0,3,2,1:T(8,128)(2,1)}, bf16[1024,...) fusion(bf16[1024,4,16,16]{0,3,2,1:T(8,128)(2,1)S(1)} %bitcast.182), kind=kLoop, calls=%fused_computation | loop fusion | bytes 22020096 | tf_op jit(solution)/shard_map/slice | solution.py:31
  61.1 73.3 %all-gather.5.cloned.1.call-done = bf16[27,256,1024]{2,1,0:T(8,128)(2,1)} async-done(((bf16[27,256,256]{2,1,0:T(8,128)(2,1)}), bf16[27,256,1024]{2,1,0:T(8,128)(2,1)}) %all-gather.5.cloned.1.call-update) | async-done | bytes 14155792 | tf_op jit(solution)/shard_map/all_gather | solution.py:45
  134.4 2.0 %convolution_bitcast_fusion.8 = f32[256,512]{0,1:T(8,128)S(1)} fusion(bf16[1024,512]{0,1:T(8,128)(2,1)} %bitcast.210, bf16[27,256,1024]{2,1,0:T(8,128)(2,1)} %all-gather.5.cloned.1.call-done), kind=kOutput, calls=%fused_computation.59 | convolution fusion | flops 268435456 | bytes 2097152 | tf_op jit(solution)/shard_map/dot_general | solution.py:34
  136.4 0.0 copy-start.12
  136.4 2.6 %convolution_bitcast_fusion.9 = f32[256,512]{0,1:T(8,128)S(1)} fusion(bf16[1024,512]{0,1:T(8,128)(2,1)} %bitcast.209, bf16[27,256,1024]{2,1,0:T(8,128)(2,1)} %all-gather.5.cloned.1.call-done), kind=kOutput, calls=%fused_computation.60 | convolution fusion | flops 268435456 | bytes 2097152 | tf_op jit(solution)/shard_map/dot_general | solution.py:34
  139.0 2.6 %fusion.12 = f32[512,256]{1,0:T(8,128)S(1)} fusion(bf16[1024,512]{0,1:T(8,128)(2,1)} %bitcast.208, bf16[27,256,1024]{2,1,0:T(8,128)(2,1)} %all-gather.5.cloned.1.call-done), kind=kOutput, calls=%fused_computation.89 | convolution fusion | flops 268435456 | bytes 2097152 | tf_op jit(solution)/shard_map/dot_general | solution.py:34
  141.6 0.0 copy-start.10
  141.6 1.9 %convolution_add_fusion.15 = f32[512,256]{1,0:T(8,128)S(1)} fusion(f32[512,256]{1,0:T(8,128)S(1)} %fusion.12, bf16[1024,512]{0,1:T(8,128)(2,1)} %bitcast.190, bf16[27,256,1024]{2,1,0:T(8,128)(2,1)} %all-gather.5.cloned.1.call-done), kind=kOutput, calls=%fused_computation.41 | convolution fusion | flops 268566528 | bytes 2621440 | tf_op jit(solution)/shard_map/dot_general | solution.py:34
  143.6 1.9 %convolution_add_fusion.14 = f32[512,256]{1,0:T(8,128)S(1)} fusion(f32[512,256]{1,0:T(8,128)S(1)} %convolution_add_fusion.15, bf16[1024,512]{0,1:T(8,128)(2,1)} %bitcast.206, bf16[27,256,1024]{2,1,0:T(8,128)(2,1)} %all-gather.5.cloned.1.call-done), kind=kOutput, calls=%fused_computation.40 | convolution fusion | flops 268566528 | bytes 2621440 | tf_op jit(solution)/shard_map/dot_general | solution.py:34
  145.5 1.9 %convolution_add_fusion.13 = f32[512,256]{1,0:T(8,128)S(1)} fusion(f32[512,256]{1,0:T(8,128)S(1)} %convolution_add_fusion.14, bf16[1024,512]{0,1:T(8,128)(2,1)} %bitcast.205, bf16[27,256,1024]{2,1,0:T(8,128)(2,1)} %all-gather.5.cloned.1.call-done), kind=kOutput, calls=%fused_computation.39 | convolution fusion | flops 268566528 | bytes 2621440 | tf_op jit(solution)/shard_map/dot_general | solution.py:34
  147.5 1.8 %convolution_add_fusion.12 = f32[512,256]{1,0:T(8,128)S(1)} fusion(f32[512,256]{1,0:T(8,128)S(1)} %convolution_add_fusion.13, bf16[1024,512]{0,1:T(8,128)(2,1)} %bitcast.189, bf16[27,256,1024]{2,1,0:T(8,128)(2,1)S(1)} %copy-done), kind=kOutput, calls=%fused_computation.38 | convolution fusion | flops 268566528 | bytes 2621440 | tf_op jit(solution)/shard_map/dot_general | solution.py:34
  149.3 1.8 %convolution_add_fusion.11 = f32[512,256]{1,0:T(8,128)S(1)} fusion(f32[512,256]{1,0:T(8,128)S(1)} %convolution_add_fusion.12, bf16[1024,512]{0,1:T(8,128)(2,1)} %bitcast.204, bf16[27,256,1024]{2,1,0:T(8,128)(2,1)S(1)} %copy-done), kind=kOutput, calls=%fused_computation.37 | convolution fusion | flops 268566528 | bytes 2621440 | tf_op jit(solution)/shard_map/dot_general | solution.py:34
  151.1 0.5 convolution_add_fusion.10
  151.6 0.5 convolution_add_fusion.9
  152.1 0.0 copy-start.6
  152.1 0.0 copy-done.14
  152.1 0.5 convolution_add_fusion.8
  152.6 0.5 convolution_add_fusion.7
  153.1 0.5 convolution_add_fusion.6
  153.6 0.5 convolution_add_fusion.5
  154.1 0.5 convolution_add_fusion.4
  154.6 0.5 convolution_add_fusion.3
  155.1 0.5 convolution_add_fusion.2
  155.6 0.0 copy-done.8
  155.6 0.5 convolution_add_fusion.1
  156.1 0.5 fusion.10
  156.6 0.5 fusion.9
  157.1 0.5 fusion.8
  157.6 0.5 fusion.7
  158.1 0.5 fusion.6
  158.5 0.5 fusion.5
  159.0 0.5 fusion.4
  159.5 0.5 fusion.3
  160.0 0.5 fusion.11
  160.5 0.9 copy.5
  (29 shorter events, 0.1 us)
Async XLA Ops:
  6.5 35.0 %all-gather.3.cloned.1.call-start = ((), (), s32[]{:S(2)}) async-start(), calls=%async_computation | async-start | bytes 1310720 | tf_op jit(solution)/shard_map/all_gather | solution.py:47
  8.4 126.0 %all-gather.5.cloned.1.call-start = ((), (), s32[]{:S(2)}) async-start(), calls=%async_computation.1 | async-start | bytes 17694720 | tf_op jit(solution)/shard_map/all_gather | solution.py:45
  42.9 4.4 %collective-permute-start.1 = (bf16[1024,1,256]{0,2,1:T(8,128)(2,1)S(1)}, bf16[1024,1,256]{0,2,1:T(8,128)(2,1)S(1)}, u32[]{:S(2)}, u32[]{:S(2)}) collective-permute-start(bf16[1024,1,256]{0,2,1:T(8,128)(2,1)S(1)} %get-tuple-element.33), channel_id=1, source_target_pairs={{4,0},{8,4},{12,8},{5,1},{9,5},{13,9},{6,2},{10,6},{14,10},{7,3},{... | collective-permute-start | bytes 1572872 | tf_op jit(solution)/shard_map/ppermute | solution.py:18
  44.1 4.6 %collective-permute-start = (bf16[1024,1,256]{0,2,1:T(8,128)(2,1)S(1)}, bf16[1024,1,256]{0,2,1:T(8,128)(2,1)S(1)}, u32[]{:S(2)}, u32[]{:S(2)}) collective-permute-start(bf16[1024,1,256]{0,2,1:T(8,128)(2,1)S(1)} %get-tuple-element.32), channel_id=1, source_target_pairs={{0,4},{4,8},{8,12},{1,5},{5,9},{9,13},{2,6},{6,10},{10,14},{3,7},{... | collective-permute-start | bytes 1572872 | tf_op jit(solution)/shard_map/ppermute | solution.py:15
  134.4 13.1 %copy-start = (bf16[27,256,1024]{2,1,0:T(8,128)(2,1)S(1)}, bf16[27,256,1024]{2,1,0:T(8,128)(2,1)}, u32[]{:S(2)}) copy-start(bf16[27,256,1024]{2,1,0:T(8,128)(2,1)} %all-gather.5.cloned.1.call-done) | copy-start | bytes 42467332
  134.4 16.7 %copy-start.16 = (bf16[1024,2,16,16]{0,3,2,1:T(8,128)(2,1)S(1)}, bf16[1024,2,16,16]{0,3,2,1:T(8,128)(2,1)}, u32[]{:S(2)}) copy-start(bf16[1024,2,16,16]{0,3,2,1:T(8,128)(2,1)} %get-tuple-element.10) | copy-start | bytes 3145732
  134.4 17.2 %copy-start.15 = (bf16[1024,2,16,16]{0,3,2,1:T(8,128)(2,1)S(1)}, bf16[1024,2,16,16]{0,3,2,1:T(8,128)(2,1)}, u32[]{:S(2)}) copy-start(bf16[1024,2,16,16]{0,3,2,1:T(8,128)(2,1)} %get-tuple-element.11) | copy-start | bytes 3145732
  134.4 17.7 %copy-start.14 = (bf16[1024,2,16,16]{0,3,2,1:T(8,128)(2,1)S(1)}, bf16[1024,2,16,16]{0,3,2,1:T(8,128)(2,1)}, u32[]{:S(2)}) copy-start(bf16[1024,2,16,16]{0,3,2,1:T(8,128)(2,1)} %get-tuple-element.12) | copy-start | bytes 3145732
  134.4 18.2 %copy-start.13 = (bf16[1024,2,16,16]{0,3,2,1:T(8,128)(2,1)S(1)}, bf16[1024,2,16,16]{0,3,2,1:T(8,128)(2,1)}, u32[]{:S(2)}) copy-start(bf16[1024,2,16,16]{0,3,2,1:T(8,128)(2,1)} %get-tuple-element.13) | copy-start | bytes 3145732
  136.4 16.7 %copy-start.12 = (bf16[1024,2,16,16]{0,3,2,1:T(8,128)(2,1)S(1)}, bf16[1024,2,16,16]{0,3,2,1:T(8,128)(2,1)}, u32[]{:S(2)}) copy-start(bf16[1024,2,16,16]{0,3,2,1:T(8,128)(2,1)} %get-tuple-element.14) | copy-start | bytes 3145732
  139.0 14.6 %copy-start.11 = (bf16[1024,2,16,16]{0,3,2,1:T(8,128)(2,1)S(1)}, bf16[1024,2,16,16]{0,3,2,1:T(8,128)(2,1)}, u32[]{:S(2)}) copy-start(bf16[1024,2,16,16]{0,3,2,1:T(8,128)(2,1)} %get-tuple-element.15) | copy-start | bytes 3145732
  141.6 12.4 %copy-start.10 = (bf16[1024,2,16,16]{0,3,2,1:T(8,128)(2,1)S(1)}, bf16[1024,2,16,16]{0,3,2,1:T(8,128)(2,1)}, u32[]{:S(2)}) copy-start(bf16[1024,2,16,16]{0,3,2,1:T(8,128)(2,1)} %get-tuple-element.16) | copy-start | bytes 3145732
  143.6 11.0 %copy-start.3 = (bf16[1024,2,16,16]{0,3,2,1:T(8,128)(2,1)S(1)}, bf16[1024,2,16,16]{0,3,2,1:T(8,128)(2,1)}, u32[]{:S(2)}) copy-start(bf16[1024,2,16,16]{0,3,2,1:T(8,128)(2,1)} %get-tuple-element.29) | copy-start | bytes 3145732
  145.5 9.6 %copy-start.9 = (bf16[1024,2,16,16]{0,3,2,1:T(8,128)(2,1)S(1)}, bf16[1024,2,16,16]{0,3,2,1:T(8,128)(2,1)}, u32[]{:S(2)}) copy-start(bf16[1024,2,16,16]{0,3,2,1:T(8,128)(2,1)} %get-tuple-element.17) | copy-start | bytes 3145732
  147.5 8.1 %copy-start.8 = (bf16[1024,2,16,16]{0,3,2,1:T(8,128)(2,1)S(1)}, bf16[1024,2,16,16]{0,3,2,1:T(8,128)(2,1)}, u32[]{:S(2)}) copy-start(bf16[1024,2,16,16]{0,3,2,1:T(8,128)(2,1)} %get-tuple-element.18) | copy-start | bytes 3145732
  149.3 6.8 %copy-start.4 = (bf16[1024,2,16,16]{0,3,2,1:T(8,128)(2,1)S(1)}, bf16[1024,2,16,16]{0,3,2,1:T(8,128)(2,1)}, u32[]{:S(2)}) copy-start(bf16[1024,2,16,16]{0,3,2,1:T(8,128)(2,1)} %get-tuple-element.19) | copy-start | bytes 3145732
  151.6 5.0 %copy-start.7 = (bf16[1024,2,16,16]{0,3,2,1:T(8,128)(2,1)S(1)}, bf16[1024,2,16,16]{0,3,2,1:T(8,128)(2,1)}, u32[]{:S(2)}) copy-start(bf16[1024,2,16,16]{0,3,2,1:T(8,128)(2,1)} %get-tuple-element.22) | copy-start | bytes 3145732
  152.1 5.0 %copy-start.6 = (bf16[1024,2,16,16]{0,3,2,1:T(8,128)(2,1)S(1)}, bf16[1024,2,16,16]{0,3,2,1:T(8,128)(2,1)}, u32[]{:S(2)}) copy-start(bf16[1024,2,16,16]{0,3,2,1:T(8,128)(2,1)} %get-tuple-element.23) | copy-start | bytes 3145732
  152.6 5.0 %copy-start.2 = (bf16[1024,2,16,16]{0,3,2,1:T(8,128)(2,1)S(1)}, bf16[1024,2,16,16]{0,3,2,1:T(8,128)(2,1)}, u32[]{:S(2)}) copy-start(bf16[1024,2,16,16]{0,3,2,1:T(8,128)(2,1)} %get-tuple-element.25) | copy-start | bytes 3145732
  153.1 5.0 %copy-start.1 = (bf16[1024,2,16,16]{0,3,2,1:T(8,128)(2,1)S(1)}, bf16[1024,2,16,16]{0,3,2,1:T(8,128)(2,1)}, u32[]{:S(2)}) copy-start(bf16[1024,2,16,16]{0,3,2,1:T(8,128)(2,1)} %get-tuple-element.28) | copy-start | bytes 3145732
  155.1 4.9 %copy-start.5 = (bf16[1024,2,16,16]{0,3,2,1:T(8,128)(2,1)S(1)}, bf16[1024,2,16,16]{0,3,2,1:T(8,128)(2,1)}, u32[]{:S(2)}) copy-start(bf16[1024,2,16,16]{0,3,2,1:T(8,128)(2,1)} %get-tuple-element.5) | copy-start | bytes 3145732
Sparse Core Ops, SparseCore 0:
  8.9 32.6 all-gather.2
  43.1 91.1 all-gather.4
where the time goes:
time: 169 us; the launch traced here: 168 us
  waiting for transfers between devices  108 us (64%)
  matrix products  25.6 us (15%)
  local copies, waits for them, and re-layouts  14.8 us (9%)
  between operations  13.9 us (8%)
  starting transfers between devices  4.4 us (3%)
    all_gather x1, waiting for transfers between devices, local(): weights = lax.all_gather(conv_weight, 'space', axis=2, tiled=True)  73.3 us
    all_gather x1, waiting for transfers between devices, local(): gathered = lax.all_gather(fields, 'chan', axis=0, tiled=True)  32.5 us
    dot_general x27, matrix products, convolve_block(): jnp.dot(weights[9 * step_x + 3 * step_y + step_z], window, preferred_elem...  25.6 us
    slice x2, local copies, waits for them, and re-layouts, convolve_block(): padded[:, step_x:step_x + depth, step_y:step_y + NY, step_z:step_z + NZ]  10.8 us
  transfers between devices with their start and end apart: 4, of which 3 were waited for; matrix products, arithmetic and copies ran while one was open for 8% of the time, Pallas kernels for 0%

commit v1 on v0

v1 whole, which is shorter than its diff:
```python
import functools

import jax
import jax.numpy as jnp
from jax import lax
from jax.experimental import pallas as pl
from jax.experimental.pallas import tpu as pltpu
from jax.sharding import PartitionSpec as P

NZ = 16
TAPS = 27
MESH = pl.DeviceIdType.MESH


def kernel(
    S, n, r, x_ref, w_ref, out_ref,
    xz, xr, xs, wv, psend, precv, xsend, xrecv, own,
    w_sem, up_sem, down_sem, z_sem, a_send, a_recv, p_send, p_recv, q_send, q_recv,
):
    depth, cells, chb = x_ref.shape
    I = r * chb
    nx = S // 2
    planes = S * depth
    s = lax.axis_index("space")
    z = lax.axis_index("chan")
    x = s // 2
    k = s % 2
    partner = x * 2 + (1 - k)

    for t in range(TAPS):
        pltpu.make_async_copy(w_ref.at[t], wv.at[:, t * I : (t + 1) * I], w_sem.at[t]).start()

    barrier = pltpu.get_barrier_semaphore()

    @pl.when(z > 0)
    def _():
        pl.semaphore_signal(barrier, inc=1, device_id={"chan": z - 1}, device_id_type=MESH)

    @pl.when(z < n - 1)
    def _():
        pl.semaphore_signal(barrier, inc=1, device_id={"chan": z + 1}, device_id_type=MESH)

    for so in range(1, S):
        pl.semaphore_signal(
            barrier, inc=1, device_id={"space": lax.rem(s + so, S)}, device_id_type=MESH
        )
    here = jnp.where(z > 0, 1, 0) + jnp.where(z < n - 1, 1, 0) + (S - 1)
    pl.semaphore_wait(barrier, here)

    def hop(src, b, p, sem, to):
        return pltpu.make_async_remote_copy(
            src_ref=src, dst_ref=xz.at[b, p], send_sem=sem, recv_sem=z_sem.at[b, p],
            device_id={"chan": to}, device_id_type=MESH,
        )

    def across(src, b, p):
        return pltpu.make_async_remote_copy(
            src_ref=src, dst_ref=xr.at[s, b % r, p], send_sem=a_send.at[b, p],
            recv_sem=a_recv.at[s, b % r, p],
            device_id={"space": b // r}, device_id_type=MESH,
        )

    def source(h, b, p):
        return x_ref.at[p] if h == 0 else xz.at[b, p]

    def up(h, p):
        return hop(source(h, z - h, p), z - h, p, up_sem.at[h, p], z + 1)

    def down(h, p):
        return hop(source(h, z + h, p), z + h, p, down_sem.at[h, p], z - 1)

    for h in range(n):
        for p in range(depth):
            if h > 0:
                @pl.when(z - h >= 0)
                def _():
                    hop(xz.at[z - h, p], z - h, p, up_sem.at[0, p], z).wait_recv()

            if h < n - 1:
                @pl.when((z - h >= 0) & (z < n - 1))
                def _():
                    up(h, p).start()

            if h > 0:
                @pl.when(z + h < n)
                def _():
                    hop(xz.at[z + h, p], z + h, p, up_sem.at[0, p], z).wait_recv()

            if h < n - 1:
                @pl.when((z + h < n) & (z > 0))
                def _():
                    down(h, p).start()

            for sign in (-1, 1) if h > 0 else (1,):
                b = z + sign * h

                @pl.when((b >= 0) & (b < n) & (b // r != s))
                def _():
                    across(source(h, b, p), b, p).start()

    rows = lax.broadcasted_iota(jnp.int32, (cells, chb), 0) % NZ
    zero_row = jnp.zeros((NZ, I), xs.dtype)
    zero_plane = jnp.zeros(xs.shape[2:], xs.dtype)
    for c in range(3):
        xs[0, c] = zero_plane
        xs[planes + 1, c] = zero_plane

        @pl.loop(1, planes + 1)
        def _(q):
            xs[q, c, :NZ, :] = zero_row
            xs[q, c, NZ + cells :, :] = zero_row

    def prepare(v, q, j):
        wide = v.astype(jnp.float32)
        before = jnp.where(rows == 0, 0.0, pltpu.roll(wide, 1, 0))
        after = jnp.where(rows == NZ - 1, 0.0, pltpu.roll(wide, cells - 1, 0))
        lanes = slice(j * chb, (j + 1) * chb)
        xs[q + 1, 0, NZ : NZ + cells, lanes] = before.astype(xs.dtype)
        xs[q + 1, 1, NZ : NZ + cells, lanes] = v
        xs[q + 1, 2, NZ : NZ + cells, lanes] = after.astype(xs.dtype)

    for j in range(r):
        @pl.when(z == s * r + j)
        def _():
            @pl.loop(0, depth)
            def _(p):
                prepare(x_ref[p], s * depth + p, j)

        @pl.when(z != s * r + j)
        def _():
            @pl.loop(0, depth)
            def _(p):
                prepare(xz[s * r + j, p], s * depth + p, j)

    @pl.loop(1, S)
    def _(so):
        src = lax.rem(s + so, S)

        @pl.loop(0, depth)
        def _(p):
            for j in range(r):
                pltpu.make_async_remote_copy(
                    src_ref=xr.at[src, j, p], dst_ref=xr.at[src, j, p],
                    send_sem=a_send.at[0, p], recv_sem=a_recv.at[src, j, p],
                    device_id={"space": src}, device_id_type=MESH,
                ).wait_recv()
                prepare(xr[src, j, p], src * depth + p, j)

    for t in range(TAPS):
        pltpu.make_async_copy(w_ref.at[t], wv.at[:, t * I : (t + 1) * I], w_sem.at[t]).wait()

    def partial(q):
        window = jnp.concatenate(
            [
                xs[q + a, c, NZ * b : NZ * b + cells, :]
                for a in range(3)
                for b in range(3)
                for c in range(3)
            ],
            axis=1,
        )
        return lax.dot_general(
            window, wv[...], (((1,), (1,)), ((), ())), preferred_element_type=jnp.float32
        )

    def to_partner(m):
        return pltpu.make_async_remote_copy(
            src_ref=psend.at[m], dst_ref=precv.at[m], send_sem=p_send.at[m],
            recv_sem=p_recv.at[m], device_id={"space": partner}, device_id_type=MESH,
        )

    def to_chip(m, there):
        return pltpu.make_async_remote_copy(
            src_ref=xsend.at[m], dst_ref=xrecv.at[m], send_sem=q_send.at[m],
            recv_sem=q_recv.at[m], device_id={"space": there}, device_id_type=MESH,
        )

    @pl.loop(0, 2 * planes // 2)
    def _(i):
        m = i // 2
        mine = i % 2
        hops = m // depth + 1
        p = m % depth
        far = lax.rem(x + hops, nx)
        core = jnp.where(mine == 1, k, 1 - k)
        total = partial((far * 2 + core) * depth + p)

        @pl.when(mine == 0)
        def _():
            psend[m] = total
            to_partner(m).start()

        @pl.when(mine == 1)
        def _():
            to_partner(m).wait_recv()

            @pl.when(hops < nx)
            def _():
                xsend[m] = total + precv[m]
                to_chip(m, far * 2 + k).start()

            @pl.when(hops == nx)
            def _():
                own[p] = total + precv[m]

    for p in range(depth):
        total = own[p]
        for hops in range(1, nx):
            m = (hops - 1) * depth + p
            to_chip(m, partner).wait_recv()
            total = total + xrecv[m]
        out_ref[p] = total.astype(out_ref.dtype)

    for h in range(n):
        for p in range(depth):
            if h < n - 1:
                @pl.when((z - h >= 0) & (z < n - 1))
                def _():
                    up(h, p).wait_send()

                @pl.when((z + h < n) & (z > 0))
                def _():
                    down(h, p).wait_send()

            for sign in (-1, 1) if h > 0 else (1,):
                b = z + sign * h

                @pl.when((b >= 0) & (b < n) & (b // r != s))
                def _():
                    across(source(h, b, p), b, p).wait_send()

    for m in range(nx * depth):
        to_partner(m).wait_send()
        if m < (nx - 1) * depth:
            to_chip(m, partner).wait_send()


def local(S, n, fields, conv_weight):
    chb, depth, cells = fields.shape
    owned, I = conv_weight.shape[1:]
    r = I // chb
    nx = S // 2
    planes = S * depth
    bf16, f32 = jnp.bfloat16, jnp.float32
    dma = pltpu.SemaphoreType.DMA
    x = jnp.transpose(fields, (1, 2, 0))
    result = pl.pallas_call(
        functools.partial(kernel, S, n, r),
        out_shape=jax.ShapeDtypeStruct((depth, cells, owned), bf16),
        in_specs=[
            pl.BlockSpec(memory_space=pltpu.VMEM),
            pl.BlockSpec(memory_space=pl.ANY),
        ],
        out_specs=pl.BlockSpec(memory_space=pltpu.VMEM),
        scratch_shapes=[
            pltpu.VMEM((n, depth, cells, chb), bf16),
            pltpu.VMEM((S, r, depth, cells, chb), bf16),
            pltpu.VMEM((planes + 2, 3, cells + 2 * NZ, I), bf16),
            pltpu.VMEM((owned, TAPS * I), bf16),
            pltpu.VMEM((nx * depth, cells, owned), f32),
            pltpu.VMEM((nx * depth, cells, owned), f32),
            pltpu.VMEM(((nx - 1) * depth, cells, owned), f32),
            pltpu.VMEM(((nx - 1) * depth, cells, owned), f32),
            pltpu.VMEM((depth, cells, owned), f32),
            dma((TAPS,)),
            dma((n, depth)),
            dma((n, depth)),
            dma((n, depth)),
            dma((n, depth)),
            dma((S, r, depth)),
            dma((nx * depth,)),
            dma((nx * depth,)),
            dma((nx * depth,)),
            dma((nx * depth,)),
        ],
        compiler_params=pltpu.CompilerParams(
            collective_id=0, has_side_effects=True, vmem_limit_bytes=50 * 1024 * 1024
        ),
    )(x, conv_weight)
    return jnp.transpose(result, (2, 0, 1))


def solution(mesh):
    return jax.shard_map(
        functools.partial(local, mesh.shape["space"], mesh.shape["chan"]),
        mesh=mesh,
        in_specs=(P("chan", ("groups", "space"), None), P(None, "chan", "space")),
        out_specs=P("chan", ("groups", "space"), None),
        check_vma=False,
    )
```

time: 169 us -> 48.3 us (0.29)
  waiting for transfers between devices: 108 us -> 0 us
  Pallas kernels: 0 us -> 44.2 us
  matrix products: 25.6 us -> 0 us
  between operations: 13.9 us -> 0.02 us
  local copies, waits for them, and re-layouts: 14.8 us -> 3.96 us
  starting transfers between devices: 4.4 us -> 0 us
    all_gather x2 -> x0, waiting for transfers between devices: 106 us -> none  [the longest x1 73.3 us: local(): weights = lax.all_gather(conv_weight, 'space', axis=2, tiled=True)]
    pallas_call x0 -> x1, Pallas kernels: none -> 44.2 us  [local(): pl.pallas_call(functools.partial(kernel, S, n, r), out_shape=jax.ShapeDty...]
    dot_general x27 -> x0, matrix products: 25.6 us -> none  [convolve_block(): jnp.dot(weights[9 * step_x + 3 * step_y + step_z], window, preferred_elem...]
    slice x3 -> x0, local copies, waits for them, and re-layouts: 12 us -> none  [the longest x2 10.8 us: convolve_block(): padded[:, step_x:step_x + depth, step_y:step_y + NY, step_z:step_z + NZ]]
    ppermute x2 -> x0, starting transfers between devices: 4.36 us -> none  [the longest x1 3.06 us: padded_2(): lax.ppermute(lax.slice_in_dim(block, block.shape[dim] - width, None, axis...]
  transfers between devices with their start and end apart: 4 -> 0, of which waited for: 3 -> 0; matrix products, arithmetic and copies ran while one was open for 8% -> 0% of each run, Pallas kernels for 0% -> 0%
where the time goes in v1:
time: 48.3 us; the launch traced here: 48.2 us
  Pallas kernels  44.2 us (92%)
  local copies, waits for them, and re-layouts  3.96 us (8%)
    pallas_call x1, Pallas kernels, local(): pl.pallas_call(functools.partial(kernel, S, n, r), out_shape=jax.ShapeDty...  44.2 us
    unnamed x3, local copies, waits for them, and re-layouts  3.1 us

profile of v1, /device:TPU:0, one launch (start us, length us, event | category | flops | bytes accessed | tf_op | source)
XLA Modules:
  0.0 48.2 jit_solution(17258314067805722025)
XLA Ops:
  0.0 1.1 %copy.3 = bf16[256,2,256]{0,2,1:T(8,128)(2,1)S(1)} copy(bf16[256,2,256]{2,1,0:T(2,128)(2,1)} %param.2) | data formatting | bytes 524288 | tf_op args[0]
  1.1 0.0 copy-start
  1.1 2.0 %copy-done = bf16[27,256,256]{2,1,0:T(8,128)(2,1)S(1)} copy-done((bf16[27,256,256]{2,1,0:T(8,128)(2,1)S(1)}, bf16[27,256,256]{2,1,0:T(8,128)(2,1)}, u32[]{:S(2)}) %copy-start) | copy-done | bytes 3538968
  3.1 44.2 %shard_map.28 = bf16[2,256,256]{2,1,0:T(8,128)(2,1)S(1)} custom-call(bf16[2,256,256]{2,1,0:T(8,128)(2,1)S(1)} %bitcast.3, bf16[27,256,256]{2,1,0:T(8,128)(2,1)S(1)} %copy-done), custom_call_target="tpu_custom_call" | custom-call | tf_op jit(solution)/shard_map/pallas_call | solution.py:247
  47.3 0.9 %copy.4 = bf16[256,2,256]{2,1,0:T(2,128)(2,1)} copy(bf16[256,2,256]{0,2,1:T(8,128)(2,1)S(1)} %bitcast.2) | data formatting | bytes 524288 | tf_op jit(solution)/shard_map/transpose | solution.py:280
Async XLA Ops:
  1.1 2.0 %copy-start = (bf16[27,256,256]{2,1,0:T(8,128)(2,1)S(1)}, bf16[27,256,256]{2,1,0:T(8,128)(2,1)}, u32[]{:S(2)}) copy-start(bf16[27,256,256]{2,1,0:T(8,128)(2,1)} %w_ref.1) | copy-start | bytes 10616836

commit v2 on v1

--- a/solution.py
+++ b/solution.py
@@ -14,7 +14,7 @@
 
 def kernel(
     S, n, r, x_ref, w_ref, out_ref,
-    xz, xr, xs, wv, psend, precv, xsend, xrecv, own,
+    xz, xr, xs, wv, psend, precv, xsend, xrecv, own, early,
     w_sem, up_sem, down_sem, z_sem, a_send, a_recv, p_send, p_recv, q_send, q_recv,
 ):
     depth, cells, chb = x_ref.shape
@@ -32,19 +32,20 @@
 
     barrier = pltpu.get_barrier_semaphore()
 
-    @pl.when(z > 0)
-    def _():
-        pl.semaphore_signal(barrier, inc=1, device_id={"chan": z - 1}, device_id_type=MESH)
-
-    @pl.when(z < n - 1)
-    def _():
-        pl.semaphore_signal(barrier, inc=1, device_id={"chan": z + 1}, device_id_type=MESH)
+    for so in range(S):
+        for step, there in ((-1, z > 0), (1, z < n - 1)):
+            @pl.when(there)
+            def _():
+                pl.semaphore_signal(
+                    barrier, inc=1, device_id={"space": lax.rem(s + so, S), "chan": z + step},
+                    device_id_type=MESH,
+                )
 
     for so in range(1, S):
         pl.semaphore_signal(
             barrier, inc=1, device_id={"space": lax.rem(s + so, S)}, device_id_type=MESH
         )
-    here = jnp.where(z > 0, 1, 0) + jnp.where(z < n - 1, 1, 0) + (S - 1)
+    here = jnp.where(z > 0, S, 0) + jnp.where(z < n - 1, S, 0) + (S - 1)
     pl.semaphore_wait(barrier, here)
 
     def hop(src, b, p, sem, to):
@@ -69,34 +70,46 @@
     def down(h, p):
         return hop(source(h, z + h, p), z + h, p, down_sem.at[h, p], z - 1)
 
-    for h in range(n):
-        for p in range(depth):
+    def slanted(h, b, p, sem, to):
+        return pltpu.make_async_remote_copy(
+            src_ref=source(h, b, p), dst_ref=xr.at[s, b % r, p], send_sem=sem,
+            recv_sem=a_recv.at[s, b % r, p],
+            device_id={"space": b // r, "chan": to}, device_id_type=MESH,
+        )
+
+    def direct(h, b, to, end):
+        return (to == end) & (b // r != s)
+
+    def forward(h, p):
+        for b, sign, end, send in ((z - h, 1, n - 1, up), (z + h, -1, 0, down)):
+            valid = (b >= 0) & (b < n)
+            relay = valid
             if h > 0:
-                @pl.when(z - h >= 0)
-                def _():
-                    hop(xz.at[z - h, p], z - h, p, up_sem.at[0, p], z).wait_recv()
+                relay = valid & ~direct(h - 1, b, z, end)
+
+                @pl.when(relay)
+                def _():
+                    hop(xz.at[b, p], b, p, up_sem.at[0, p], z).wait_recv()
 
             if h < n - 1:
-                @pl.when((z - h >= 0) & (z < n - 1))
-                def _():
-                    up(h, p).start()
-
-            if h > 0:
-                @pl.when(z + h < n)
-                def _():
-                    hop(xz.at[z + h, p], z + h, p, up_sem.at[0, p], z).wait_recv()
-
-            if h < n - 1:
-                @pl.when((z + h < n) & (z > 0))
-                def _():
-                    down(h, p).start()
-
-            for sign in (-1, 1) if h > 0 else (1,):
-                b = z + sign * h
-
-                @pl.when((b >= 0) & (b < n) & (b // r != s))
+                straight = direct(h, b, z + sign, end)
+
+                @pl.when(valid & (z != end) & ~straight)
+                def _():
+                    send(h, p).start()
+
+                @pl.when(valid & (z != end) & straight)
+                def _():
+                    sem = (up_sem if sign == 1 else down_sem).at[h, p]
+                    slanted(h, b, p, sem, z + sign).start()
+
+            if h > 0 or sign == 1:
+                @pl.when(relay & (b // r != s))
                 def _():
                     across(source(h, b, p), b, p).start()
+
+    for p in range(depth):
+        forward(0, p)
 
     rows = lax.broadcasted_iota(jnp.int32, (cells, chb), 0) % NZ
     zero_row = jnp.zeros((NZ, I), xs.dtype)
@@ -119,49 +132,94 @@
         xs[q + 1, 1, NZ : NZ + cells, lanes] = v
         xs[q + 1, 2, NZ : NZ + cells, lanes] = after.astype(xs.dtype)
 
-    for j in range(r):
-        @pl.when(z == s * r + j)
-        def _():
-            @pl.loop(0, depth)
-            def _(p):
+    for h in range(1, n - 1):
+        for p in range(depth):
+            forward(h, p)
+
+    def fetch_own(p):
+        for j in range(r):
+            @pl.when(z == s * r + j)
+            def _():
                 prepare(x_ref[p], s * depth + p, j)
 
-        @pl.when(z != s * r + j)
-        def _():
-            @pl.loop(0, depth)
-            def _(p):
+            @pl.when(z != s * r + j)
+            def _():
                 prepare(xz[s * r + j, p], s * depth + p, j)
 
-    @pl.loop(1, S)
-    def _(so):
-        src = lax.rem(s + so, S)
-
-        @pl.loop(0, depth)
-        def _(p):
-            for j in range(r):
-                pltpu.make_async_remote_copy(
-                    src_ref=xr.at[src, j, p], dst_ref=xr.at[src, j, p],
-                    send_sem=a_send.at[0, p], recv_sem=a_recv.at[src, j, p],
-                    device_id={"space": src}, device_id_type=MESH,
-                ).wait_recv()
-                prepare(xr[src, j, p], src * depth + p, j)
+    def fetch(src, p):
+        for j in range(r):
+            pltpu.make_async_remote_copy(
+                src_ref=xr.at[src, j, p], dst_ref=xr.at[src, j, p],
+                send_sem=a_send.at[0, p], recv_sem=a_recv.at[src, j, p],
+                device_id={"space": src}, device_id_type=MESH,
+            ).wait_recv()
+            prepare(xr[src, j, p], src * depth + p, j)
+
+    def fetch_far(p):
+        @pl.loop(0, S)
+        def _(src):
+            @pl.when(src // 2 != x)
+            def _():
+                fetch(src, p)
 
     for t in range(TAPS):
         pltpu.make_async_copy(w_ref.at[t], wv.at[:, t * I : (t + 1) * I], w_sem.at[t]).wait()
 
-    def partial(q):
+    def terms(q, taps):
         window = jnp.concatenate(
             [
                 xs[q + a, c, NZ * b : NZ * b + cells, :]
-                for a in range(3)
+                for a in taps
                 for b in range(3)
                 for c in range(3)
             ],
             axis=1,
         )
+        if len(taps) == 3:
+            held = wv[...]
+        else:
+            held = jnp.concatenate([wv[:, 9 * I * a : 9 * I * (a + 1)] for a in taps], axis=1)
         return lax.dot_general(
-            window, wv[...], (((1,), (1,)), ((), ())), preferred_element_type=jnp.float32
-        )
+            window, held, (((1,), (1,)), ((), ())), preferred_element_type=jnp.float32
+        )
+
+    def parity(p):
+        return tuple(a for a in range(3) if (p + a - 1) % 2 == 0)
+
+    def target(hops, mine):
+        far = lax.rem(x + hops, nx)
+        return far * 2 + jnp.where(mine == 1, k, 1 - k)
+
+    def start_early():
+        fetch_own(0)
+        fetch(partner, 0)
+        fetch_far(0)
+
+        @pl.loop(0, 2 * (nx - 1))
+        def _(i):
+            dest = target(i // 2 + 1, i % 2)
+            for p in range(depth):
+                early[i, p] = terms(dest * depth + p, parity(p))
+
+    last = jnp.abs(z - s // r) if r == 1 else n - 1
+
+    @pl.when(last < n - 1)
+    def _():
+        start_early()
+
+    forward(n - 1, 0)
+
+    @pl.when(last == n - 1)
+    def _():
+        start_early()
+
+    for p in range(1, depth):
+        forward(n - 1, p)
+
+    for p in range(1, depth):
+        fetch_own(p)
+        fetch(partner, p)
+        fetch_far(p)
 
     def to_partner(m):
         return pltpu.make_async_remote_copy(
@@ -175,16 +233,7 @@
             recv_sem=q_recv.at[m], device_id={"space": there}, device_id_type=MESH,
         )
 
-    @pl.loop(0, 2 * planes // 2)
-    def _(i):
-        m = i // 2
-        mine = i % 2
-        hops = m // depth + 1
-        p = m % depth
-        far = lax.rem(x + hops, nx)
-        core = jnp.where(mine == 1, k, 1 - k)
-        total = partial((far * 2 + core) * depth + p)
-
+    def finish(m, p, hops, mine, total):
         @pl.when(mine == 0)
         def _():
             psend[m] = total
@@ -197,11 +246,27 @@
             @pl.when(hops < nx)
             def _():
                 xsend[m] = total + precv[m]
-                to_chip(m, far * 2 + k).start()
+                to_chip(m, target(hops, 1)).start()
 
             @pl.when(hops == nx)
             def _():
                 own[p] = total + precv[m]
+
+    for p in range(depth - 1, -1, -1):
+        rest = tuple(a for a in range(3) if a not in parity(p))
+        @pl.loop(0, 2 * (nx - 1))
+        def _(i):
+            hops = i // 2 + 1
+            mine = i % 2
+            total = early[i, p] + terms(target(hops, mine) * depth + p, rest)
+            finish((hops - 1) * depth + p, p, hops, mine, total)
+
+    @pl.loop(0, 2 * depth)
+    def _(i):
+        p = i // 2
+        mine = i % 2
+        total = terms(target(nx, mine) * depth + p, (0, 1, 2))
+        finish((nx - 1) * depth + p, p, nx, mine, total)
 
     for p in range(depth):
         total = own[p]
@@ -222,12 +287,15 @@
                 def _():
                     down(h, p).wait_send()
 
-            for sign in (-1, 1) if h > 0 else (1,):
-                b = z + sign * h
-
-                @pl.when((b >= 0) & (b < n) & (b // r != s))
-                def _():
-                    across(source(h, b, p), b, p).wait_send()
+            for b, sign, end in ((z - h, 1, n - 1), (z + h, -1, 0)):
+                relay = (b >= 0) & (b < n) & (b // r != s)
+                if h > 0:
+                    relay = relay & ~direct(h - 1, b, z, end)
+
+                if h > 0 or sign == 1:
+                    @pl.when(relay)
+                    def _():
+                        across(source(h, b, p), b, p).wait_send()
 
     for m in range(nx * depth):
         to_partner(m).wait_send()
@@ -262,6 +330,7 @@
             pltpu.VMEM(((nx - 1) * depth, cells, owned), f32),
             pltpu.VMEM(((nx - 1) * depth, cells, owned), f32),
             pltpu.VMEM((depth, cells, owned), f32),
+            pltpu.VMEM((2 * (nx - 1), depth, cells, owned), f32),
             dma((TAPS,)),
             dma((n, depth)),
             dma((n, depth)),
@@ -274,7 +343,7 @@
             dma((nx * depth,)),
         ],
         compiler_params=pltpu.CompilerParams(
-            collective_id=0, has_side_effects=True, vmem_limit_bytes=50 * 1024 * 1024
+            collective_id=0, has_side_effects=True, vmem_limit_bytes=62 * 1024 * 1024
         ),
     )(x, conv_weight)
     return jnp.transpose(result, (2, 0, 1))

time: 48.3 us -> 45.2 us (0.936)
  Pallas kernels: 44.2 us -> 41.4 us
    pallas_call x1, Pallas kernels: 44.2 us -> 41.4 us  [local(): pl.pallas_call(functools.partial(kernel, S, n, r), out_shape=jax.ShapeDty...]
    unnamed x3 -> x1, local copies, waits for them, and re-layouts: 3.1 us -> 1.81 us
    transpose x1, local copies, waits for them, and re-layouts: 0.87 us -> 1.82 us  [local(): return jnp.transpose(result, (2, 0, 1))]
where the time goes in v2:
time: 45.2 us; the launch traced here: 45 us
  Pallas kernels  41.4 us (92%)
  local copies, waits for them, and re-layouts  3.63 us (8%)
    pallas_call x1, Pallas kernels, local(): pl.pallas_call(functools.partial(kernel, S, n, r), out_shape=jax.ShapeDty...  41.4 us
    transpose x1, local copies, waits for them, and re-layouts, local(): return jnp.transpose(result, (2, 0, 1))  1.82 us
    unnamed x1, local copies, waits for them, and re-layouts  1.81 us

profile of v2, /device:TPU:0, one launch (start us, length us, event | category | flops | bytes accessed | tf_op | source)
XLA Modules:
  0.0 45.0 jit_solution(18291014079210874460)
XLA Ops:
  0.0 1.8 %copy.3 = bf16[256,2,256]{0,2,1:T(8,128)(2,1)} copy(bf16[256,2,256]{2,1,0:T(2,128)(2,1)} %param.2) | data formatting | bytes 524288 | tf_op args[0]
  1.8 41.4 %shard_map.28 = bf16[2,256,256]{2,1,0:T(8,128)(2,1)} custom-call(bf16[2,256,256]{2,1,0:T(8,128)(2,1)} %bitcast.3, bf16[27,256,256]{2,1,0:T(8,128)(2,1)} %w_ref.1), custom_call_target="tpu_custom_call" | custom-call | tf_op jit(solution)/shard_map/pallas_call | solution.py:315
  43.2 1.8 %copy.4 = bf16[256,2,256]{2,1,0:T(2,128)(2,1)} copy(bf16[256,2,256]{0,2,1:T(8,128)(2,1)} %bitcast.2) | data formatting | bytes 524288 | tf_op jit(solution)/shard_map/transpose | solution.py:349

commit v3 on v2

v3 whole, which is shorter than its diff:
```python
import functools

import jax
import jax.numpy as jnp
from jax import lax
from jax.experimental import pallas as pl
from jax.experimental.pallas import tpu as pltpu
from jax.sharding import PartitionSpec as P

NZ = 16
TAPS = 27
MESH = pl.DeviceIdType.MESH


def kernel(
    S, n, r, x_ref, w_ref, out_ref,
    xz, xr, xs, wv, psend, precv, xsend, xrecv, own,
    w_sem, up_sem, down_sem, z_sem, a_send, a_recv, p_send, p_recv, q_send, q_recv,
):
    depth, cells, chb = x_ref.shape
    I = r * chb
    nx = S // 2
    planes = S * depth
    s = lax.axis_index("space")
    z = lax.axis_index("chan")
    x = s // 2
    k = s % 2
    partner = x * 2 + (1 - k)

    for t in range(TAPS):
        pltpu.make_async_copy(w_ref.at[t], wv.at[:, t * I : (t + 1) * I], w_sem.at[t]).start()

    barrier = pltpu.get_barrier_semaphore()

    for so in range(S):
        for step, there in ((-1, z > 0), (1, z < n - 1)):
            @pl.when(there)
            def _():
                pl.semaphore_signal(
                    barrier, inc=1, device_id={"space": lax.rem(s + so, S), "chan": z + step},
                    device_id_type=MESH,
                )

    for so in range(1, S):
        pl.semaphore_signal(
            barrier, inc=1, device_id={"space": lax.rem(s + so, S)}, device_id_type=MESH
        )
    here = jnp.where(z > 0, S, 0) + jnp.where(z < n - 1, S, 0) + (S - 1)
    pl.semaphore_wait(barrier, here)

    split = cells // 2 + NZ
    spans = ((0, split), (split, cells - split))
    rows_out = cells // 2

    def part(ref, u):
        return ref.at[u % depth, pl.ds(*spans[u // depth])]

    def hop(src, b, p, sem, to):
        return pltpu.make_async_remote_copy(
            src_ref=src, dst_ref=part(xz.at[b], p), send_sem=sem, recv_sem=z_sem.at[b, p],
            device_id={"chan": to}, device_id_type=MESH,
        )

    def across(src, b, p):
        return pltpu.make_async_remote_copy(
            src_ref=src, dst_ref=part(xr.at[s, b % r], p), send_sem=a_send.at[b, p],
            recv_sem=a_recv.at[s, b % r, p],
            device_id={"space": b // r}, device_id_type=MESH,
        )

    def source(h, b, p):
        return part(x_ref, p) if h == 0 else part(xz.at[b], p)

    def up(h, p):
        return hop(source(h, z - h, p), z - h, p, up_sem.at[h, p], z + 1)

    def down(h, p):
        return hop(source(h, z + h, p), z + h, p, down_sem.at[h, p], z - 1)

    def slanted(h, b, p, sem, to):
        return pltpu.make_async_remote_copy(
            src_ref=source(h, b, p), dst_ref=part(xr.at[s, b % r], p), send_sem=sem,
            recv_sem=a_recv.at[s, b % r, p],
            device_id={"space": b // r, "chan": to}, device_id_type=MESH,
        )

    def direct(h, b, to, end):
        return (to == end) & (b // r != s)

    def forward(h, p):
        for b, sign, end, send in ((z - h, 1, n - 1, up), (z + h, -1, 0, down)):
            valid = (b >= 0) & (b < n)
            relay = valid
            if h > 0:
                relay = valid & ~direct(h - 1, b, z, end)

                @pl.when(relay)
                def _():
                    hop(part(xz.at[b], p), b, p, up_sem.at[0, p], z).wait_recv()

            if h < n - 1:
                straight = direct(h, b, z + sign, end)

                @pl.when(valid & (z != end) & ~straight)
                def _():
                    send(h, p).start()

                @pl.when(valid & (z != end) & straight)
                def _():
                    sem = (up_sem if sign == 1 else down_sem).at[h, p]
                    slanted(h, b, p, sem, z + sign).start()

            if h > 0 or sign == 1:
                @pl.when(relay & (b // r != s))
                def _():
                    across(source(h, b, p), b, p).start()

    for p in range(2 * depth):
        forward(0, p)

    zero_row = jnp.zeros((NZ, I), xs.dtype)
    zero_plane = jnp.zeros(xs.shape[2:], xs.dtype)
    for c in range(3):
        xs[0, c] = zero_plane
        xs[planes + 1, c] = zero_plane

        @pl.loop(1, planes + 1)
        def _(q):
            xs[q, c, :NZ, :] = zero_row
            xs[q, c, NZ + cells :, :] = zero_row

    def prepare(ref, u, q, j):
        v = part(ref, u)[...]
        start, size = spans[u // depth]
        rows = lax.broadcasted_iota(jnp.int32, (size, chb), 0) % NZ
        wide = v.astype(jnp.float32)
        before = jnp.where(rows == 0, 0.0, pltpu.roll(wide, 1, 0))
        after = jnp.where(rows == NZ - 1, 0.0, pltpu.roll(wide, size - 1, 0))
        lanes = slice(j * chb, (j + 1) * chb)
        to = slice(NZ + start, NZ + start + size)
        xs[q + 1, 0, to, lanes] = before.astype(xs.dtype)
        xs[q + 1, 1, to, lanes] = v
        xs[q + 1, 2, to, lanes] = after.astype(xs.dtype)

    for h in range(1, n - 1):
        for p in range(2 * depth):
            forward(h, p)

    def fetch_half(half):
        for p in range(depth):
            u = half * depth + p
            for j in range(r):
                @pl.when(z == s * r + j)
                def _():
                    prepare(x_ref, u, s * depth + p, j)

                @pl.when(z != s * r + j)
                def _():
                    prepare(xz.at[s * r + j], u, s * depth + p, j)

            @pl.loop(1, S)
            def _(so):
                src = lax.rem(s + so, S)
                for j in range(r):
                    view = part(xr.at[src, j], u)
                    pltpu.make_async_remote_copy(
                        src_ref=view, dst_ref=view,
                        send_sem=a_send.at[0, u], recv_sem=a_recv.at[src, j, u],
                        device_id={"space": src}, device_id_type=MESH,
                    ).wait_recv()
                    prepare(xr.at[src, j], u, src * depth + p, j)

    for t in range(TAPS):
        pltpu.make_async_copy(w_ref.at[t], wv.at[:, t * I : (t + 1) * I], w_sem.at[t]).wait()

    def partial(dest, half):
        window = jnp.concatenate(
            [
                jnp.concatenate(
                    [
                        xs[
                            dest * depth + p + a, c,
                            NZ * b + half * rows_out : NZ * b + (half + 1) * rows_out, :,
                        ]
                        for p in range(depth)
                    ],
                    axis=0,
                )
                for a in range(3)
                for b in range(3)
                for c in range(3)
            ],
            axis=1,
        )
        return lax.dot_general(
            window, wv[...], (((1,), (1,)), ((), ())), preferred_element_type=jnp.float32
        )

    def target(hops, mine):
        far = lax.rem(x + hops, nx)
        return far * 2 + jnp.where(mine == 1, k, 1 - k)

    def half_of(ref, m, half):
        return ref.at[m, half]

    def to_partner(m, half):
        return pltpu.make_async_remote_copy(
            src_ref=half_of(psend, m, half), dst_ref=half_of(precv, m, half),
            send_sem=p_send.at[m, half], recv_sem=p_recv.at[m, half],
            device_id={"space": partner}, device_id_type=MESH,
        )

    def to_chip(m, half, there):
        return pltpu.make_async_remote_copy(
            src_ref=half_of(xsend, m, half), dst_ref=half_of(xrecv, m, half),
            send_sem=q_send.at[m, half], recv_sem=q_recv.at[m, half],
            device_id={"space": there}, device_id_type=MESH,
        )

    def reduce_half(half, first, stop):
        @pl.loop(2 * first, 2 * stop)
        def _(i):
            m = i // 2
            mine = i % 2
            total = partial(target(m + 1, mine), half)

            @pl.when(mine == 0)
            def _():
                psend[m, half] = total
                to_partner(m, half).start()

            @pl.when(mine == 1)
            def _():
                to_partner(m, half).wait_recv()
                if first < nx - 1:
                    xsend[m, half] = total + precv[m, half]
                    to_chip(m, half, target(m + 1, 1)).start()
                else:
                    own[half] = total + precv[m, half]

    for p in range(depth):
        forward(n - 1, p)
    fetch_half(0)
    reduce_half(0, 0, nx - 1)
    for p in range(depth, 2 * depth):
        forward(n - 1, p)
    fetch_half(1)
    reduce_half(1, 0, nx - 1)
    for half in range(2):
        reduce_half(half, nx - 1, nx)

    for half in range(2):
        total = own[half]
        for m in range(nx - 1):
            to_chip(m, half, partner).wait_recv()
            total = total + xrecv[m, half]
        for p in range(depth):
            out_ref[p, half * rows_out : (half + 1) * rows_out, :] = total[
                p * rows_out : (p + 1) * rows_out
            ].astype(out_ref.dtype)

    for h in range(n):
        for p in range(2 * depth):
            if h < n - 1:
                @pl.when((z - h >= 0) & (z < n - 1))
                def _():
                    up(h, p).wait_send()

                @pl.when((z + h < n) & (z > 0))
                def _():
                    down(h, p).wait_send()

            for b, sign, end in ((z - h, 1, n - 1), (z + h, -1, 0)):
                relay = (b >= 0) & (b < n) & (b // r != s)
                if h > 0:
                    relay = relay & ~direct(h - 1, b, z, end)

                if h > 0 or sign == 1:
                    @pl.when(relay)
                    def _():
                        across(source(h, b, p), b, p).wait_send()

    for m in range(nx):
        for half in range(2):
            to_partner(m, half).wait_send()
            if m < nx - 1:
                to_chip(m, half, partner).wait_send()


def local(S, n, fields, conv_weight):
    chb, depth, cells = fields.shape
    owned, I = conv_weight.shape[1:]
    r = I // chb
    nx = S // 2
    planes = S * depth
    bf16, f32 = jnp.bfloat16, jnp.float32
    dma = pltpu.SemaphoreType.DMA
    x = jnp.transpose(fields, (1, 2, 0))
    result = pl.pallas_call(
        functools.partial(kernel, S, n, r),
        out_shape=jax.ShapeDtypeStruct((depth, cells, owned), bf16),
        in_specs=[
            pl.BlockSpec(memory_space=pltpu.VMEM),
            pl.BlockSpec(memory_space=pl.ANY),
        ],
        out_specs=pl.BlockSpec(memory_space=pltpu.VMEM),
        scratch_shapes=[
            pltpu.VMEM((n, depth, cells, chb), bf16),
            pltpu.VMEM((S, r, depth, cells, chb), bf16),
            pltpu.VMEM((planes + 2, 3, cells + 2 * NZ, I), bf16),
            pltpu.VMEM((owned, TAPS * I), bf16),
            pltpu.VMEM((nx, 2, depth * cells // 2, owned), f32),
            pltpu.VMEM((nx, 2, depth * cells // 2, owned), f32),
            pltpu.VMEM((nx - 1, 2, depth * cells // 2, owned), f32),
            pltpu.VMEM((nx - 1, 2, depth * cells // 2, owned), f32),
            pltpu.VMEM((2, depth * cells // 2, owned), f32),
            dma((TAPS,)),
            dma((n, 2 * depth)),
            dma((n, 2 * depth)),
            dma((n, 2 * depth)),
            dma((n, 2 * depth)),
            dma((S, r, 2 * depth)),
            dma((nx, 2)),
            dma((nx, 2)),
            dma((nx, 2)),
            dma((nx, 2)),
        ],
        compiler_params=pltpu.CompilerParams(
            collective_id=0, has_side_effects=True, vmem_limit_bytes=62 * 1024 * 1024
        ),
    )(x, conv_weight)
    return jnp.transpose(result, (2, 0, 1))


def solution(mesh):
    return jax.shard_map(
        functools.partial(local, mesh.shape["space"], mesh.shape["chan"]),
        mesh=mesh,
        in_specs=(P("chan", ("groups", "space"), None), P(None, "chan", "space")),
        out_specs=P("chan", ("groups", "space"), None),
        check_vma=False,
    )
```

time: 45.2 us -> 44.1 us (0.976)
  Pallas kernels: 41.4 us -> 40.3 us
    pallas_call x1, Pallas kernels: 41.4 us -> 40.3 us  [local(): pl.pallas_call(functools.partial(kernel, S, n, r), out_shape=jax.ShapeDty...]
where the time goes in v3:
time: 44.1 us; the launch traced here: 43.9 us
  Pallas kernels  40.3 us (91%)
  local copies, waits for them, and re-layouts  3.63 us (8%)
    pallas_call x1, Pallas kernels, local(): pl.pallas_call(functools.partial(kernel, S, n, r), out_shape=jax.ShapeDty...  40.3 us
    transpose x1, local copies, waits for them, and re-layouts, local(): return jnp.transpose(result, (2, 0, 1))  1.82 us
    unnamed x1, local copies, waits for them, and re-layouts  1.81 us

profile of v3, /device:TPU:0, one launch (start us, length us, event | category | flops | bytes accessed | tf_op | source)
XLA Modules:
  0.0 43.9 jit_solution(1144211434072969632)
XLA Ops:
  0.0 1.8 %copy.3 = bf16[256,2,256]{0,2,1:T(8,128)(2,1)} copy(bf16[256,2,256]{2,1,0:T(2,128)(2,1)} %param.2) | data formatting | bytes 524288 | tf_op args[0]
  1.8 40.3 %shard_map.28 = bf16[2,256,256]{2,1,0:T(8,128)(2,1)} custom-call(bf16[2,256,256]{2,1,0:T(8,128)(2,1)} %bitcast.3, bf16[27,256,256]{2,1,0:T(8,128)(2,1)} %w_ref.1), custom_call_target="tpu_custom_call" | custom-call | tf_op jit(solution)/shard_map/pallas_call | solution.py:299
  42.1 1.8 %copy.4 = bf16[256,2,256]{2,1,0:T(2,128)(2,1)} copy(bf16[256,2,256]{0,2,1:T(8,128)(2,1)} %bitcast.2) | data formatting | bytes 524288 | tf_op jit(solution)/shard_map/transpose | solution.py:332

commit v4 on v3

--- a/solution.py
+++ b/solution.py
@@ -92,7 +92,7 @@
             valid = (b >= 0) & (b < n)
             relay = valid
             if h > 0:
-                relay = valid & ~direct(h - 1, b, z, end)
+                relay = valid & (z != end)
 
                 @pl.when(relay)
                 def _():
@@ -142,9 +142,10 @@
         xs[q + 1, 1, to, lanes] = v
         xs[q + 1, 2, to, lanes] = after.astype(xs.dtype)
 
-    for h in range(1, n - 1):
-        for p in range(2 * depth):
-            forward(h, p)
+    for half in range(2):
+        for h in range(1, n - 1):
+            for p in range(depth):
+                forward(h, half * depth + p)
 
     def fetch_half(half):
         for p in range(depth):
@@ -153,6 +154,12 @@
                 @pl.when(z == s * r + j)
                 def _():
                     prepare(x_ref, u, s * depth + p, j)
+
+                b = s * r + j
+
+                @pl.when(((z == 0) & (b > 0)) | ((z == n - 1) & (b < n - 1)))
+                def _():
+                    hop(part(xz.at[b], u), b, u, up_sem.at[0, u], z).wait_recv()
 
                 @pl.when(z != s * r + j)
                 def _():
@@ -238,12 +245,8 @@
                 else:
                     own[half] = total + precv[m, half]
 
-    for p in range(depth):
-        forward(n - 1, p)
     fetch_half(0)
     reduce_half(0, 0, nx - 1)
-    for p in range(depth, 2 * depth):
-        forward(n - 1, p)
     fetch_half(1)
     reduce_half(1, 0, nx - 1)
     for half in range(2):

time: 44.1 us -> 43.4 us (0.984)
  Pallas kernels: 40.3 us -> 39.5 us
    pallas_call x1, Pallas kernels: 40.3 us -> 39.5 us  [local(): pl.pallas_call(functools.partial(kernel, S, n, r), out_shape=jax.ShapeDty...]
where the time goes in v4:
time: 43.4 us; the launch traced here: 43.2 us
  Pallas kernels  39.5 us (91%)
  local copies, waits for them, and re-layouts  3.63 us (8%)
    pallas_call x1, Pallas kernels, local(): pl.pallas_call(functools.partial(kernel, S, n, r), out_shape=jax.ShapeDty...  39.5 us
    transpose x1, local copies, waits for them, and re-layouts, local(): return jnp.transpose(result, (2, 0, 1))  1.82 us
    unnamed x1, local copies, waits for them, and re-layouts  1.81 us

profile of v4, /device:TPU:0, one launch (start us, length us, event | category | flops | bytes accessed | tf_op | source)
XLA Modules:
  0.0 43.2 jit_solution(10540651312086534855)
XLA Ops:
  0.0 1.8 %copy.3 = bf16[256,2,256]{0,2,1:T(8,128)(2,1)} copy(bf16[256,2,256]{2,1,0:T(2,128)(2,1)} %param.2) | data formatting | bytes 524288 | tf_op args[0]
  1.8 39.5 %shard_map.28 = bf16[2,256,256]{2,1,0:T(8,128)(2,1)} custom-call(bf16[2,256,256]{2,1,0:T(8,128)(2,1)} %bitcast.3, bf16[27,256,256]{2,1,0:T(8,128)(2,1)} %w_ref.1), custom_call_target="tpu_custom_call" | custom-call | tf_op jit(solution)/shard_map/pallas_call | solution.py:302
  41.4 1.8 %copy.4 = bf16[256,2,256]{2,1,0:T(2,128)(2,1)} copy(bf16[256,2,256]{0,2,1:T(8,128)(2,1)} %bitcast.2) | data formatting | bytes 524288 | tf_op jit(solution)/shard_map/transpose | solution.py:335
